TPU v7x, 256 devices: a whole 4x4x8 slice. The times are simulated.
256 devices in a mesh: replica: 32 (over z, y_hi, core), fsdp: 8 (over y_lo, x).
Axes of the slice: x: 4, y: 4 (y_hi: 2, y_lo: 2; y = y_hi * 2 + y_lo), z: 8, core: 2. Of those that a mesh axis runs over, the one named last changes fastest.
Arguments:
- params: float32 [32, 128, 5120], P('replica', 'fsdp'), may hold values from -0.012 to 0.012
- tracker: float32 [32, 128, 5120], P('replica', 'fsdp'), may hold values from -2.1 to 2.1
- last_grad: float32 [32, 128, 5120], P('replica', 'fsdp'), may hold values from -2.1 to 2.1
- first_moment: float32 [32, 128, 5120], P('replica', 'fsdp'), may hold values from -1.8 to 1.8
- second_moment: float32 [32, 128, 5120], P('replica', 'fsdp'), may hold values from 0.02 to 0.5
- local_grads: bfloat16 [4, 32, 8, 128, 5120], P(None, 'replica', 'fsdp'), may hold values from -6 to 6
Outputs:
- param_change: float32 [32, 128, 5120], P('replica', 'fsdp')
- moment_one: float32 [32, 128, 5120], P('replica', 'fsdp')
- moment_two: float32 [32, 128, 5120], P('replica', 'fsdp')
All inputs are finite; a program needn't handle non-finite values.
Results may differ from a plain program's by a relative error of at most 0.0003.
Values sent between devices are 32-bit elements; how exact they have to be, the bound alone decides.
A program may use at most 64 MiB of HBM per device.

v0:
```python
import jax
import jax.numpy as jnp
from jax import lax
from jax.sharding import PartitionSpec as P

LEARNING_RATE = 0.001
BETA_ONE = 0.9
BETA_TWO = 0.999
EPSILON = 1e-08


def shifted(value, axis, steps):
    count = lax.axis_size(axis)
    pairs = [(source, (source + steps) % count) for source in range(count)]
    return lax.ppermute(value, axis, pairs)


def per_device(params, tracker, last_grad, first_moment, second_moment, local_grads):
    initial = params[0]
    weights = initial
    tracking = tracker[0]
    previous = last_grad[0]
    moment_one = first_moment[0]
    moment_two = second_moment[0]
    span_bits = lax.axis_size("replica").bit_length() - 1
    inverse_count = 1.0 / lax.axis_size("fsdp")
    step_count = local_grads.shape[0]
    for iteration in range(step_count):
        grad_total = lax.psum_scatter(
            local_grads[iteration, 0, 0].astype(jnp.float32),
            "fsdp",
            scatter_dimension=0,
            tiled=True,
        )
        mean_grad = grad_total * inverse_count
        distance = 2 ** (iteration % span_bits)
        remote_weights, remote_tracking = shifted((weights, tracking), "replica", distance)
        weights = 0.5 * (weights + remote_weights)
        tracking = 0.5 * (tracking + remote_tracking) + mean_grad - previous
        previous = mean_grad
        moment_one = BETA_ONE * moment_one + (1.0 - BETA_ONE) * tracking
        moment_two = BETA_TWO * moment_two + (1.0 - BETA_TWO) * tracking * tracking
        weights = weights - LEARNING_RATE * moment_one / (jnp.sqrt(moment_two) + EPSILON)
    change = (weights - initial) / LEARNING_RATE
    return (change[None], moment_one[None], moment_two[None])


def solution(mesh):
    in_specs = (
        P("replica", "fsdp", None),
        P("replica", "fsdp", None),
        P("replica", "fsdp", None),
        P("replica", "fsdp", None),
        P("replica", "fsdp", None),
        P(None, "replica", "fsdp", None, None),
    )
    out_specs = (P("replica", "fsdp", None), P("replica", "fsdp", None), P("replica", "fsdp", None))
    return jax.shard_map(
        per_device, mesh=mesh, in_specs=in_specs, out_specs=out_specs, check_vma=False
    )
```

profile of v0, /device:TPU:16, one launch (start us, length us, event | category | flops | bytes accessed | tf_op | source)
XLA Modules:
  0.0 235.1 jit_solution(4258179607481156557)
XLA Ops:
  7.2 0.0 reduce-scatter.5.cloned.1.call-start
  7.2 6.9 %bitcast_convert_fusion.2 = (f32[128,5120]{1,0:T(8,128)}, f32[128,5120]{1,0:T(8,128)}, f32[128,5120]{1,0:T(8,128)}, f32[128,5120]{1,0:T(8,128)}) fusion(bf16[4,1,1,128,5120]{4,3,2,1,0:T(8,128)(2,1)} %param.11), kind=kLoop, calls=%fused_computation.2 | loop fusion | flops 2621440 | bytes 15728640 | tf_op jit(solution)/shard_map/convert_element_type | solution.py:30
  14.1 0.0 reduce-scatter.5.cloned.1.call-update
  14.1 0.0 reduce-scatter.7.cloned.1.call-start
  14.1 0.7 reduce-scatter.7.cloned.1.call-update
  14.8 0.0 reduce-scatter.9.cloned.1.call-start
  14.9 0.0 copy-start.6
  14.9 0.6 reduce-scatter.9.cloned.1.call-update
  15.6 0.0 reduce-scatter.11.cloned.1.call-start
  15.6 0.5 reduce-scatter.11.cloned.1.call-update
  16.2 0.1 collective-permute-start
  16.3 1.8 collective-permute-start.1
  18.1 6.2 %collective-permute-done = f32[16,5120]{1,0:T(8,128)S(1)} collective-permute-done((f32[16,5120]{1,0:T(8,128)S(1)}, f32[16,5120]{1,0:T(8,128)S(1)}, u32[]{:S(2)}, u32[]{:S(2)}) %collective-permute-start) | collective-permute-done | bytes 327712 | tf_op jit(solution)/shard_map/ppermute | solution.py:15
  24.2 3.5 %collective-permute-done.1 = f32[16,5120]{1,0:T(8,128)S(1)} collective-permute-done((f32[16,5120]{1,0:T(8,128)S(1)}, f32[16,5120]{1,0:T(8,128)S(1)}, u32[]{:S(2)}, u32[]{:S(2)}) %collective-permute-start.1) | collective-permute-done | bytes 327712 | tf_op jit(solution)/shard_map/ppermute | solution.py:15
  27.8 35.9 %reduce-scatter.5.cloned.1.call-done = f32[16,5120]{1,0:T(8,128)} async-done(((f32[128,5120]{1,0:T(8,128)}), f32[16,5120]{1,0:T(8,128)}) %reduce-scatter.5.cloned.1.call-update) | async-done | bytes 327696 | tf_op jit(solution)/shard_map/reduce_scatter | solution.py:29
  63.7 1.3 divide_subtract_fusion.2
  65.0 2.0 collective-permute-start.3
  67.1 2.7 %collective-permute-start.2 = (f32[16,5120]{1,0:T(8,128)S(1)}, f32[16,5120]{1,0:T(8,128)}, u32[]{:S(2)}, u32[]{:S(2)}) collective-permute-start(f32[16,5120]{1,0:T(8,128)S(1)} %get-tuple-element.10), channel_id=1, source_target_pairs={{0,16},{8,24},{16,32},{24,40},{32,48},{40,56},{48,64},{56,72},{64,... | collective-permute-start | bytes 983048 | tf_op jit(solution)/shard_map/ppermute | solution.py:15
  69.8 42.5 %reduce-scatter.7.cloned.1.call-done = f32[16,5120]{1,0:T(8,128)} async-done(((f32[128,5120]{1,0:T(8,128)}), f32[16,5120]{1,0:T(8,128)}) %reduce-scatter.7.cloned.1.call-update) | async-done | bytes 327696 | tf_op jit(solution)/shard_map/reduce_scatter | solution.py:29
  112.3 1.5 divide_subtract_fusion.1
  113.8 1.7 collective-permute-start.5
  115.5 46.0 %reduce-scatter.9.cloned.1.call-done = f32[16,5120]{1,0:T(8,128)} async-done(((f32[128,5120]{1,0:T(8,128)}), f32[16,5120]{1,0:T(8,128)}) %reduce-scatter.9.cloned.1.call-update) | async-done | bytes 327696 | tf_op jit(solution)/shard_map/reduce_scatter | solution.py:29
  161.6 1.0 add_subtract_fusion.1
  162.6 2.5 %collective-permute-start.7 = (f32[16,5120]{1,0:T(8,128)S(1)}, f32[16,5120]{1,0:T(8,128)S(1)}, u32[]{:S(2)}, u32[]{:S(2)}) collective-permute-start(f32[16,5120]{1,0:T(8,128)S(1)} %add_subtract_fusion.1), channel_id=1, source_target_pairs={{0,64},{8,72},{16,80},{24,88},{32,96},{40,104},{48,112},{56,120},{... | collective-permute-start | bytes 983048 | tf_op jit(solution)/shard_map/ppermute | solution.py:15
  165.1 1.6 collective-permute-start.4
  166.7 42.9 %reduce-scatter.11.cloned.1.call-done = f32[16,5120]{1,0:T(8,128)} async-done(((f32[128,5120]{1,0:T(8,128)}), f32[16,5120]{1,0:T(8,128)}) %reduce-scatter.11.cloned.1.call-update) | async-done | bytes 327696 | tf_op jit(solution)/shard_map/reduce_scatter | solution.py:29
  209.6 2.0 fusion.5
  211.6 0.9 fusion.4
  212.5 0.2 divide_subtract_fusion
  212.7 3.0 %collective-permute-start.6 = (f32[16,5120]{1,0:T(8,128)S(1)}, f32[16,5120]{1,0:T(8,128)S(1)}, u32[]{:S(2)}, u32[]{:S(2)}) collective-permute-start(f32[16,5120]{1,0:T(8,128)S(1)} %divide_subtract_fusion), channel_id=1, source_target_pairs={{0,64},{8,72},{16,80},{24,88},{32,96},{40,104},{48,112},{56,120},{... | collective-permute-start | bytes 983048 | tf_op jit(solution)/shard_map/ppermute | solution.py:15
  215.7 11.9 %collective-permute-done.6 = f32[16,5120]{1,0:T(8,128)S(1)} collective-permute-done((f32[16,5120]{1,0:T(8,128)S(1)}, f32[16,5120]{1,0:T(8,128)S(1)}, u32[]{:S(2)}, u32[]{:S(2)}) %collective-permute-start.6) | collective-permute-done | bytes 327712 | tf_op jit(solution)/shard_map/ppermute | solution.py:15
  227.5 1.0 multiply_bitcast_fusion
  (18 shorter events, 0.0 us)
Async XLA Ops:
  7.2 56.5 %reduce-scatter.5.cloned.1.call-start = ((), (), s32[]{:S(2)}) async-start(), calls=%async_computation.4 | async-start | bytes 2949120 | tf_op jit(solution)/shard_map/reduce_scatter | solution.py:29
  14.1 98.2 %reduce-scatter.7.cloned.1.call-start = ((), (), s32[]{:S(2)}) async-start(), calls=%async_computation.5 | async-start | bytes 2949120 | tf_op jit(solution)/shard_map/reduce_scatter | solution.py:29
  14.8 146.7 %reduce-scatter.9.cloned.1.call-start = ((), (), s32[]{:S(2)}) async-start(), calls=%async_computation.6 | async-start | bytes 2949120 | tf_op jit(solution)/shard_map/reduce_scatter | solution.py:29
  14.9 1.3 copy-start.2
  14.9 1.4 copy-start.6
  14.9 48.8 %copy-start = (f32[1,16,5120]{2,1,0:T(8,128)S(1)}, f32[1,16,5120]{2,1,0:T(8,128)}, u32[]{:S(2)}) copy-start(f32[1,16,5120]{2,1,0:T(8,128)} %param.10) | copy-start | bytes 983044
  14.9 48.8 %copy-start.1 = (f32[1,16,5120]{2,1,0:T(8,128)S(1)}, f32[1,16,5120]{2,1,0:T(8,128)}, u32[]{:S(2)}) copy-start(f32[1,16,5120]{2,1,0:T(8,128)} %param.9) | copy-start | bytes 983044
  14.9 48.8 %copy-start.5 = (f32[1,16,5120]{2,1,0:T(8,128)S(1)}, f32[1,16,5120]{2,1,0:T(8,128)}, u32[]{:S(2)}) copy-start(f32[1,16,5120]{2,1,0:T(8,128)} %param.8) | copy-start | bytes 983044
  15.6 194.0 %reduce-scatter.11.cloned.1.call-start = ((), (), s32[]{:S(2)}) async-start(), calls=%async_computation.7 | async-start | bytes 2949120 | tf_op jit(solution)/shard_map/reduce_scatter | solution.py:29
  16.2 8.1 %collective-permute-start = (f32[16,5120]{1,0:T(8,128)S(1)}, f32[16,5120]{1,0:T(8,128)S(1)}, u32[]{:S(2)}, u32[]{:S(2)}) collective-permute-start(f32[16,5120]{1,0:T(8,128)S(1)} %bitcast.45), channel_id=1, source_target_pairs={{0,8},{8,16},{16,24},{24,32},{32,40},{40,48},{48,56},{56,64},{64,7... | collective-permute-start | bytes 983048 | tf_op jit(solution)/shard_map/ppermute | solution.py:15
  16.3 11.5 %collective-permute-start.1 = (f32[16,5120]{1,0:T(8,128)S(1)}, f32[16,5120]{1,0:T(8,128)S(1)}, u32[]{:S(2)}, u32[]{:S(2)}) collective-permute-start(f32[16,5120]{1,0:T(8,128)S(1)} %bitcast.46), channel_id=1, source_target_pairs={{0,8},{8,16},{16,24},{24,32},{32,40},{40,48},{48,56},{56,64},{64,7... | collective-permute-start | bytes 983048 | tf_op jit(solution)/shard_map/ppermute | solution.py:15
  63.7 48.6 %copy-start.3 = (f32[16,5120]{1,0:T(8,128)S(1)}, f32[16,5120]{1,0:T(8,128)}, u32[]{:S(2)}) copy-start(f32[16,5120]{1,0:T(8,128)} %reduce-scatter.5.cloned.1.call-done) | copy-start | bytes 983044
  65.0 47.3 %collective-permute-start.3 = (f32[16,5120]{1,0:T(8,128)S(1)}, f32[16,5120]{1,0:T(8,128)S(1)}, u32[]{:S(2)}, u32[]{:S(2)}) collective-permute-start(f32[16,5120]{1,0:T(8,128)S(1)} %get-tuple-element.11), channel_id=1, source_target_pairs={{0,16},{8,24},{16,32},{24,40},{32,48},{40,56},{48,64},{56,72},{64,... | collective-permute-start | bytes 983048 | tf_op jit(solution)/shard_map/ppermute | solution.py:15
  67.1 45.2 %collective-permute-start.2 = (f32[16,5120]{1,0:T(8,128)S(1)}, f32[16,5120]{1,0:T(8,128)}, u32[]{:S(2)}, u32[]{:S(2)}) collective-permute-start(f32[16,5120]{1,0:T(8,128)S(1)} %get-tuple-element.10), channel_id=1, source_target_pairs={{0,16},{8,24},{16,32},{24,40},{32,48},{40,56},{48,64},{56,72},{64,... | collective-permute-start | bytes 983048 | tf_op jit(solution)/shard_map/ppermute | solution.py:15
  112.3 49.2 %copy-start.4 = (f32[16,5120]{1,0:T(8,128)S(1)}, f32[16,5120]{1,0:T(8,128)}, u32[]{:S(2)}) copy-start(f32[16,5120]{1,0:T(8,128)} %reduce-scatter.7.cloned.1.call-done) | copy-start | bytes 983044
  113.8 47.7 %collective-permute-start.5 = (f32[16,5120]{1,0:T(8,128)S(1)}, f32[16,5120]{1,0:T(8,128)S(1)}, u32[]{:S(2)}, u32[]{:S(2)}) collective-permute-start(f32[16,5120]{1,0:T(8,128)S(1)} %get-tuple-element.9), channel_id=1, source_target_pairs={{0,32},{8,40},{16,48},{24,56},{32,64},{40,72},{48,80},{56,88},{64,... | collective-permute-start | bytes 983048 | tf_op jit(solution)/shard_map/ppermute | solution.py:15
  162.6 47.0 %collective-permute-start.7 = (f32[16,5120]{1,0:T(8,128)S(1)}, f32[16,5120]{1,0:T(8,128)S(1)}, u32[]{:S(2)}, u32[]{:S(2)}) collective-permute-start(f32[16,5120]{1,0:T(8,128)S(1)} %add_subtract_fusion.1), channel_id=1, source_target_pairs={{0,64},{8,72},{16,80},{24,88},{32,96},{40,104},{48,112},{56,120},{... | collective-permute-start | bytes 983048 | tf_op jit(solution)/shard_map/ppermute | solution.py:15
  165.1 47.3 %collective-permute-start.4 = (f32[16,5120]{1,0:T(8,128)S(1)}, f32[16,5120]{1,0:T(8,128)S(1)}, u32[]{:S(2)}, u32[]{:S(2)}) collective-permute-start(f32[16,5120]{1,0:T(8,128)S(1)} %get-tuple-element.8), channel_id=1, source_target_pairs={{0,32},{8,40},{16,48},{24,56},{32,64},{40,72},{48,80},{56,88},{64,... | collective-permute-start | bytes 983048 | tf_op jit(solution)/shard_map/ppermute | solution.py:15
  212.7 14.9 %collective-permute-start.6 = (f32[16,5120]{1,0:T(8,128)S(1)}, f32[16,5120]{1,0:T(8,128)S(1)}, u32[]{:S(2)}, u32[]{:S(2)}) collective-permute-start(f32[16,5120]{1,0:T(8,128)S(1)} %divide_subtract_fusion), channel_id=1, source_target_pairs={{0,64},{8,72},{16,80},{24,88},{32,96},{40,104},{48,112},{56,120},{... | collective-permute-start | bytes 983048 | tf_op jit(solution)/shard_map/ppermute | solution.py:15
Sparse Core Ops, SparseCore 0:
  14.2 49.4 reduce-scatter.4
  66.2 46.0 reduce-scatter.6
  114.9 46.6 reduce-scatter.8
  164.0 45.5 reduce-scatter.10
where the time goes:
time: 235 us
  waiting for transfers between devices  191 us (81%)
  starting transfers between devices  15.6 us (7%)
  other arithmetic  14.8 us (6%)
  between operations  13.8 us (6%)
    reduce_scatter x4, waiting for transfers between devices, per_device(): lax.psum_scatter(local_grads[iteration, 0, 0].astype(jnp.float32), 'fsdp'...  167 us
    ppermute x8, waiting for transfers between devices, shifted(): return lax.ppermute(value, axis, pairs)  21.6 us
    ppermute x8, starting transfers between devices, shifted(): return lax.ppermute(value, axis, pairs)  15.5 us
    convert_element_type x1, other arithmetic, per_device(): local_grads[iteration, 0, 0].astype(jnp.float32)  6.86 us
  transfers between devices with their start and end apart: 12, of which 7 were waited for; matrix products, arithmetic and copies ran while one was open for 3% of the time, Pallas kernels for 0%

commit v1 on v0

v1 whole, which is shorter than its diff:
```python
import functools

import jax
import jax.numpy as jnp
from jax import lax
from jax.experimental import pallas as pl
from jax.experimental.pallas import tpu as pltpu
from jax.sharding import PartitionSpec as P

LEARNING_RATE = 0.001
BETA_ONE = 0.9
BETA_TWO = 0.999
EPSILON = 1e-08

MESH = pl.DeviceIdType.MESH
NX = 4
CHUNKS = 4
LEAD = 1


def item_order(steps, chunks):
    half = max(1, chunks // 2)
    groups = [range(0, half), range(half, chunks)]
    order = [(k, c) for group in groups for k in range(steps - 1) for c in group]
    return order + [(steps - 1, c) for c in range(chunks)]


def kernel(
    steps, replicas, order, width,
    params, tracker, last_grad, first_moment, second_moment, grads,
    out_change, out_one, out_two,
    gbuf, state, tw, twr, s1, sx, q, ra, rx, rd, re, rc,
    load_sem, state_sem, out_sem, send_sem, recv_sem, gsend_sem, grecv_sem,
):
    f32 = jnp.float32
    chunks = width // s1.shape[-1]
    cw = s1.shape[-1]
    r = lax.axis_index("replica")
    f = lax.axis_index("fsdp")
    y = f // NX
    x = lax.rem(f, NX)
    xm = lax.rem(x + NX - 1, NX)
    xp = lax.rem(x + 1, NX)
    x2 = lax.rem(x + 2, NX)
    oy = 1 - y

    def block(bx, by):
        return by * NX + bx

    to_xm = (r, block(xm, y))
    to_xp = (r, block(xp, y))
    to_y = (r, block(x, oy))
    shifts = [2 ** (k % (replicas.bit_length() - 1)) for k in range(steps)]

    barrier = pltpu.get_barrier_semaphore()
    feeders = [to_xm, to_xp, to_y] + [(lax.rem(r + replicas - s, replicas), f) for s in shifts]
    for dev in feeders:
        pl.semaphore_signal(barrier, inc=1, device_id=dev, device_id_type=MESH)

    def cols(c):
        return pl.ds(c * cw, cw)

    def state_loads(c):
        src = [tracker, params, last_grad, first_moment, second_moment]
        dst = [tw.at[0, c, 0], tw.at[0, c, 1], state.at[c, 0], state.at[c, 1], state.at[c, 2]]
        return [
            pltpu.make_async_copy(a.at[:, cols(c)], b, state_sem.at[c, n])
            for n, (a, b) in enumerate(zip(src, dst))
        ]

    def grad_load(i):
        k, c = order[i]
        return pltpu.make_async_copy(grads.at[k, :, :, cols(c)], gbuf.at[i], load_sem.at[i])

    grad_load(0).start()
    for c in range(chunks):
        for cp in state_loads(c)[:2]:
            cp.start()
    for i in range(1, len(order)):
        grad_load(i).start()
    for c in range(chunks):
        for cp in state_loads(c)[2:]:
            cp.start()

    sent = []

    def send(i, n, src, dst, dev):
        cp = pltpu.make_async_remote_copy(
            src_ref=src, dst_ref=dst, send_sem=send_sem.at[i, n], recv_sem=recv_sem.at[i, n],
            device_id=dev, device_id_type=MESH,
        )
        cp.start()
        sent.append(cp)

    def arrived(i, n, dst):
        pltpu.make_async_copy(dst, dst, recv_sem.at[i, n]).wait()

    def gossip(k, c):
        return pltpu.make_async_remote_copy(
            src_ref=tw.at[k, c], dst_ref=twr.at[k, c], send_sem=gsend_sem.at[k, c], recv_sem=grecv_sem.at[k, c],
            device_id=(lax.rem(r + shifts[k], replicas), f), device_id_type=MESH,
        )

    def raw(i, blk):
        return gbuf[i, blk].astype(f32)

    def fill(i):
        grad_load(i).wait()
        s1[i] = raw(i, block(x2, oy))
        sx[i, 0, 0:16] = raw(i, block(xm, oy))
        sx[i, 0, 16:24] = raw(i, block(xm, y))[8:16]
        sx[i, 1, 0:16] = raw(i, block(xp, oy))
        sx[i, 1, 16:24] = raw(i, block(xp, y))[0:8]

    def phase_one(i):
        send(i, 0, s1.at[i], ra.at[i], to_y)
        send(i, 1, sx.at[i, 0], rx.at[i, 0], to_xm)
        send(i, 2, sx.at[i, 1], rx.at[i, 1], to_xp)

    def phase_two(i):
        arrived(i, 0, ra.at[i])
        ra[i] = ra[i] + raw(i, block(x2, y))
        arrived(i, 1, rx.at[i, 0])
        arrived(i, 2, rx.at[i, 1])
        send(i, 3, ra.at[i, 0:8], rd.at[i, 0], to_xm)
        send(i, 4, ra.at[i, 8:16], rd.at[i, 1], to_xp)
        q[i] = raw(i, block(x, oy)) + rx[i, 0, 0:16] + rx[i, 1, 0:16]
        send(i, 5, q.at[i], re.at[i], to_y)

    def phase_three(i):
        arrived(i, 3, rd.at[i, 0])
        rd[i, 0] = rd[i, 0] + raw(i, block(xm, y))[0:8]
        send(i, 6, rd.at[i, 0], rc.at[i, 0], to_xm)
        arrived(i, 4, rd.at[i, 1])
        rd[i, 1] = rd[i, 1] + raw(i, block(xp, y))[8:16]
        send(i, 7, rd.at[i, 1], rc.at[i, 1], to_xp)

    def phase_four(i):
        k, c = order[i]
        arrived(i, 5, re.at[i])
        arrived(i, 6, rc.at[i, 0])
        arrived(i, 7, rc.at[i, 1])
        if k == 0:
            for cp in state_loads(c)[2:]:
                cp.wait()
        gossip(k, c).wait_recv()
        own = raw(i, block(x, y))
        for h in range(2):
            rows = slice(8 * h, 8 * h + 8)
            near, far = (rc[i, 0], rx[i, 1, 16:24]) if h == 0 else (rx[i, 0, 16:24], rc[i, 1])
            mean = (own[rows] + near + far + re[i, rows]) * (1.0 / 8.0)
            track = 0.5 * (tw[k, c, 0, rows] + twr[k, c, 0, rows]) + mean - state[c, 0, rows]
            one = BETA_ONE * state[c, 1, rows] + (1.0 - BETA_ONE) * track
            two = BETA_TWO * state[c, 2, rows] + (1.0 - BETA_TWO) * track * track
            weights = 0.5 * (tw[k, c, 1, rows] + twr[k, c, 1, rows])
            weights = weights - LEARNING_RATE * one / (jnp.sqrt(two) + EPSILON)
            if k + 1 < steps:
                state[c, 0, rows] = mean
                state[c, 1, rows] = one
                state[c, 2, rows] = two
                tw[k + 1, c, 0, rows] = track
                tw[k + 1, c, 1, rows] = weights
            else:
                state[c, 0, rows] = (weights - tw[0, c, 1, rows]) / LEARNING_RATE
                state[c, 1, rows] = one
                state[c, 2, rows] = two
        if k + 1 < steps:
            cp = gossip(k + 1, c)
            cp.start()
        else:
            for n, out in enumerate((out_change, out_one, out_two)):
                pltpu.make_async_copy(state.at[c, n], out.at[:, cols(c)], out_sem.at[c, n]).start()

    count = len(order)
    fill(0)
    pl.semaphore_wait(barrier, len(feeders))
    phase_one(0)
    for c in range(chunks):
        for cp in state_loads(c)[:2]:
            cp.wait()
        gossip(0, c).start()
    for i in range(1, LEAD):
        fill(i)
        phase_one(i)
    for t in range(LEAD, count + 2 + LEAD):
        if t < count:
            fill(t)
            phase_one(t)
        if 0 <= t - LEAD < count:
            phase_two(t - LEAD)
        if 0 <= t - LEAD - 1 < count:
            phase_three(t - LEAD - 1)
        if 0 <= t - LEAD - 2 < count:
            phase_four(t - LEAD - 2)

    for cp in sent:
        cp.wait_send()
    for k in range(steps):
        for c in range(chunks):
            gossip(k, c).wait_send()
    for c in range(chunks):
        for n, out in enumerate((out_change, out_one, out_two)):
            pltpu.make_async_copy(state.at[c, n], out.at[:, cols(c)], out_sem.at[c, n]).wait()


def per_device(params, tracker, last_grad, first_moment, second_moment, local_grads):
    rows, width = params.shape[1:]
    steps = local_grads.shape[0]
    shards = lax.axis_size("fsdp")
    replicas = lax.axis_size("replica")
    order = item_order(steps, CHUNKS)
    count = len(order)
    cw = width // CHUNKS
    f32 = jnp.float32
    block = jax.ShapeDtypeStruct((rows, width), f32)
    any_spec = pl.BlockSpec(memory_space=pl.ANY)
    change, one, two = pl.pallas_call(
        functools.partial(kernel, steps, replicas, order, width),
        out_shape=(block, block, block),
        in_specs=[any_spec] * 6,
        out_specs=(any_spec,) * 3,
        scratch_shapes=[
            pltpu.VMEM((count, shards, rows, cw), jnp.bfloat16),
            pltpu.VMEM((CHUNKS, 3, rows, cw), f32),
            pltpu.VMEM((steps, CHUNKS, 2, rows, cw), f32),
            pltpu.VMEM((steps, CHUNKS, 2, rows, cw), f32),
            pltpu.VMEM((count, 16, cw), f32),
            pltpu.VMEM((count, 2, 24, cw), f32),
            pltpu.VMEM((count, 16, cw), f32),
            pltpu.VMEM((count, 16, cw), f32),
            pltpu.VMEM((count, 2, 24, cw), f32),
            pltpu.VMEM((count, 2, 8, cw), f32),
            pltpu.VMEM((count, 16, cw), f32),
            pltpu.VMEM((count, 2, 8, cw), f32),
            pltpu.SemaphoreType.DMA((count,)),
            pltpu.SemaphoreType.DMA((CHUNKS, 5)),
            pltpu.SemaphoreType.DMA((CHUNKS, 3)),
            pltpu.SemaphoreType.DMA((count, 8)),
            pltpu.SemaphoreType.DMA((count, 8)),
            pltpu.SemaphoreType.DMA((steps, CHUNKS)),
            pltpu.SemaphoreType.DMA((steps, CHUNKS)),
        ],
        compiler_params=pltpu.CompilerParams(
            collective_id=0, has_side_effects=True, vmem_limit_bytes=60 << 20
        ),
        name="gossip_window",
    )(
        params[0], tracker[0], last_grad[0], first_moment[0], second_moment[0],
        local_grads.reshape(steps, shards, rows, width),
    )
    return change[None], one[None], two[None]


def solution(mesh):
    in_specs = (P("replica", "fsdp", None),) * 5 + (P(None, "replica", "fsdp", None, None),)
    out_specs = (P("replica", "fsdp", None),) * 3
    return jax.shard_map(
        per_device, mesh=mesh, in_specs=in_specs, out_specs=out_specs, check_vma=False
    )
```

time: 235 us -> 105 us (0.45)
  the two profiles are of different devices: /device:TPU:16 before, /device:TPU:8 now
where the time goes in v1:
time: 105 us
  Pallas kernels  98.7 us (94%)
  local copies, waits for them, and re-layouts  5.15 us (5%)
    pallas_call x1, Pallas kernels, per_device(): pl.pallas_call(functools.partial(kernel, steps, replicas, order, width),...  98.7 us
    unnamed x3, local copies, waits for them, and re-layouts  5.15 us

profile of v1, /device:TPU:8, one launch (start us, length us, event | category | flops | bytes accessed | tf_op | source)
XLA Modules:
  0.0 104.5 jit_solution(3636378527641309635)
XLA Ops:
  0.6 98.7 %gossip_window.1 = (f32[16,5120]{1,0:T(8,128)}, f32[16,5120]{1,0:T(8,128)}, f32[16,5120]{1,0:T(8,128)}) custom-call(f32[16,5120]{1,0:T(8,128)} %bitcast.13, f32[16,5120]{1,0:T(8,128)} %bitcast.14, f32[16,5120]{1,0:T(8,128)} %bitcast.15, f32[16,5120]{1,0:T(8,128)} %bitcast.16, f32[16,5120]{1,0:T(8,128)} %bitcast.17, bf16[4,8,16,5120]{3,2,1,0:T(8,128)(2,1)} %bitcast.9), custom_call_target="tpu_custom_call" | custom-call | tf_op jit(solution)/shard_map/gossip_window/pallas_call | solution.py:217
  99.4 1.7 %copy.12 = f32[1,16,5120]{2,1,0:T(8,128)} copy(f32[1,16,5120]{2,1,0:T(8,128)} %bitcast.12) | data formatting | bytes 655360
  101.1 1.7 %copy.13 = f32[1,16,5120]{2,1,0:T(8,128)} copy(f32[1,16,5120]{2,1,0:T(8,128)} %bitcast.11) | data formatting | bytes 655360
  102.8 1.7 %copy.14 = f32[1,16,5120]{2,1,0:T(8,128)} copy(f32[1,16,5120]{2,1,0:T(8,128)} %bitcast.10) | data formatting | bytes 655360

commit v2 on v0

v2 whole, which is shorter than its diff:
```python
import functools

import jax
import jax.numpy as jnp
from jax import lax
from jax.experimental import pallas as pl
from jax.experimental.pallas import tpu as pltpu
from jax.sharding import PartitionSpec as P

LEARNING_RATE = 0.001
BETA_ONE = 0.9
BETA_TWO = 0.999
EPSILON = 1e-08

MESH = pl.DeviceIdType.MESH
RELAYED = (8,)
NX = 4
WIDTHS = [1152, 1152, 1024, 1024, 768]
ITEMS = [
    (0, 4), (0, 2), (1, 4), (2, 4), (1, 2), (2, 2), (0, 1), (0, 0), (1, 1), (0, 3), (2, 1), (1, 0), (1, 3),
    (2, 3), (2, 0), (3, 2), (3, 0), (3, 1), (3, 4), (3, 3),
]
X_FIRST = [4, 5, 11]
PROGRAM = [
    (0, 2), (1, 0), (1, 1), (1, 2), (1, 3), (0, 4), (0, 1), (2, 0), (0, 3), (2, 1), (1, 4), (3, 0), (2, 2),
    (3, 1), (2, 4), (1, 5), (1, 6), (4, 0), (3, 2), (4, 1), (2, 5), (3, 4), (2, 3), (0, 0), (2, 6), (1, 7),
    (4, 2), (3, 5), (3, 3), (3, 6), (4, 4), (1, 8), (1, 9), (4, 3), (2, 7), (4, 6), (1, 10), (4, 5), (2, 8),
    (3, 7), (5, 4), (2, 9), (1, 11), (4, 7), (3, 8), (2, 10), (3, 9), (2, 11), (1, 12), (5, 2), (4, 8), (3,
    10), (1, 13), (3, 11), (1, 14), (4, 9), (2, 12), (4, 10), (1, 15), (4, 11), (2, 14), (3, 12), (2, 13), (1,
    16), (5, 1), (3, 14), (1, 17), (3, 13), (4, 12), (1, 18), (2, 15), (4, 14), (1, 19), (4, 13), (2, 18), (2,
    16), (2, 17), (5, 0), (3, 15), (2, 19), (3, 16), (5, 3), (3, 17), (3, 18), (4, 15), (3, 19), (4, 16), (4,
    17), (4, 18), (4, 19),
]
FINISH_TILES = 2


def kernel(
    steps, replicas, shards, chunks,
    params, tracker, last_grad, first_moment, second_moment, grads,
    out_track, out_mix, out_one, out_two,
    gbuf, state, tw, twr, last, s1, sx, q, ra, rx, rd, re, rc,
    load_sem, state_sem, out_sem, send_sem, recv_sem, gsend_sem, grecv_sem, hop, hsend_sem, hrecv_sem,
):
    f32 = jnp.float32
    r = lax.axis_index("replica")
    f = lax.axis_index("fsdp")
    y = f // NX
    x = lax.rem(f, NX)
    xm = lax.rem(x + NX - 1, NX)
    xp = lax.rem(x + 1, NX)
    x2 = lax.rem(x + 2, NX)
    oy = 1 - y

    def block(bx, by):
        return by * NX + bx

    to_xm = (r, block(xm, y))
    to_xp = (r, block(xp, y))
    to_y = (r, block(x, oy))
    sides = ((xm, to_xm), (xp, to_xp))
    low, high = slice(0, 8), slice(8, 16)
    shifts = [2 ** (k % (replicas.bit_length() - 1)) for k in range(steps)]
    hops = [shifts[k] // 2 if shifts[k] in RELAYED else shifts[k] for k in range(steps)]

    barrier = pltpu.get_barrier_semaphore()
    feeders = [to_xm, to_xp, to_y]
    feeders += [(lax.rem(r + replicas - s, replicas), f) for s in sorted(set(hops))]
    for dev in feeders:
        pl.semaphore_signal(barrier, inc=1, device_id=dev, device_id_type=MESH)

    def cols(c):
        return pl.ds(chunks[c][0], chunks[c][1])

    def state_load(c, n):
        src = (tracker, params, last_grad, first_moment, second_moment)[n]
        dst = tw.at[0, n, :, cols(c)] if n < 2 else state.at[n - 2, :, cols(c)]
        return pltpu.make_async_copy(src.at[:, cols(c)], dst, state_sem.at[c, n])

    def grad_load(i):
        k, c = ITEMS[i]
        return pltpu.make_async_copy(grads.at[k, :, :, cols(c)], gbuf.at[k, :, :, cols(c)], load_sem.at[i])

    sent = []

    def send(i, n, src, dst, dev):
        cp = pltpu.make_async_remote_copy(
            src_ref=src, dst_ref=dst, send_sem=send_sem.at[i, n], recv_sem=recv_sem.at[i, n],
            device_id=dev, device_id_type=MESH,
        )
        cp.start()
        sent.append(cp)

    def arrived(i, n, dst):
        pltpu.make_async_copy(dst, dst, recv_sem.at[i, n]).wait()

    def gossip(k, c, final=True):
        direct = final and hops[k] == shifts[k]
        src = tw if direct or not final else hop
        dst = twr if final else hop
        sems = (gsend_sem, grecv_sem) if final else (hsend_sem, hrecv_sem)
        return pltpu.make_async_remote_copy(
            src_ref=(src.at[k] if src is tw else src.at[0]).at[:, :, cols(c)],
            dst_ref=(dst.at[k] if dst is twr else dst.at[0]).at[:, :, cols(c)],
            send_sem=sems[0].at[k, c], recv_sem=sems[1].at[k, c],
            device_id=(lax.rem(r + hops[k], replicas), f), device_id_type=MESH,
        )

    def start_gossip(k, c):
        gossip(k, c, hops[k] == shifts[k]).start()

    def relay(c):
        for k in range(steps):
            if hops[k] != shifts[k]:
                gossip(k, c, False).wait_recv()
                gossip(k, c).start()

    def raw(i, bx, by):
        k, c = ITEMS[i]
        return gbuf[k, block(bx, by), :, cols(c)].astype(f32)

    def fill(i):
        k, c = ITEMS[i]
        cc = cols(c)
        grad_load(i).wait()
        if i in X_FIRST:
            for n, (bx, _) in enumerate(sides):
                ours, theirs = (low, high) if n == 0 else (high, low)
                for b, by in enumerate((y, oy)):
                    sx[k, n, 8 * b : 8 * b + 8, cc] = raw(i, x2, by)[ours]
                    sx[k, n, 16 + 8 * b : 24 + 8 * b, cc] = raw(i, bx, by)[theirs]
        else:
            s1[k, :, cc] = raw(i, x2, oy)
            for n, (bx, _) in enumerate(sides):
                sx[k, n, 0:16, cc] = raw(i, bx, oy)
                sx[k, n, 16:24, cc] = raw(i, bx, y)[high if n == 0 else low]

    def phase_one(i):
        k, c = ITEMS[i]
        cc = cols(c)
        if i in X_FIRST:
            for n, (_, dev) in enumerate(sides):
                send(i, 3 + n, sx.at[k, n, 0:16, cc], rx.at[k, n, 0:16, cc], dev)
            for n, (_, dev) in enumerate(sides):
                send(i, 1 + n, sx.at[k, n, 16:32, cc], rx.at[k, n, 16:32, cc], dev)
        else:
            send(i, 0, s1.at[k, :, cc], ra.at[k, :, cc], to_y)
            for n, (_, dev) in enumerate(sides):
                send(i, 1 + n, sx.at[k, n, 0:24, cc], rx.at[k, n, 0:24, cc], dev)

    def phase_two(i):
        k, c = ITEMS[i]
        cc = cols(c)
        if i in X_FIRST:
            for n, (bx, dev) in enumerate(sides):
                arrived(i, 3 + n, rx.at[k, n, 0:16, cc])
                for b, by in enumerate((y, oy)):
                    rows = slice(8 * b, 8 * b + 8)
                    rx[k, n, rows, cc] = rx[k, n, rows, cc] + raw(i, bx, by)[low if n == 0 else high]
                send(i, 6 + n, rx.at[k, n, 0:16, cc], rc.at[k, n, :, cc], dev)
        else:
            arrived(i, 0, ra.at[k, :, cc])
            ra[k, :, cc] = ra[k, :, cc] + raw(i, x2, y)
            for n, (_, dev) in enumerate(sides):
                send(i, 3 + n, ra.at[k, 8 * n : 8 * n + 8, cc], rd.at[k, n, :, cc], dev)
            for n in range(2):
                arrived(i, 1 + n, rx.at[k, n, 0:24, cc])
            q[k, :, cc] = raw(i, x, oy) + rx[k, 0, 0:16, cc] + rx[k, 1, 0:16, cc]
            send(i, 5, q.at[k, :, cc], re.at[k, :, cc], to_y)

    def phase_three(i):
        k, c = ITEMS[i]
        cc = cols(c)
        if i in X_FIRST:
            for n in range(2):
                arrived(i, 1 + n, rx.at[k, n, 16:32, cc])
                arrived(i, 6 + n, rc.at[k, n, :, cc])
            mine = raw(i, x, oy)
            q[k, 0:8, cc] = mine[low] + rc[k, 0, 8:16, cc] + rx[k, 1, 24:32, cc]
            q[k, 8:16, cc] = mine[high] + rx[k, 0, 24:32, cc] + rc[k, 1, 8:16, cc]
            send(i, 5, q.at[k, :, cc], re.at[k, :, cc], to_y)
        else:
            for n, (bx, dev) in enumerate(sides):
                arrived(i, 3 + n, rd.at[k, n, :, cc])
                rd[k, n, :, cc] = rd[k, n, :, cc] + raw(i, bx, y)[low if n == 0 else high]
                send(i, 6 + n, rd.at[k, n, :, cc], rc.at[k, n, 0:8, cc], dev)

    def phase_four(i):
        k, c = ITEMS[i]
        cc = cols(c)
        if i not in X_FIRST:
            for n in range(2):
                arrived(i, 6 + n, rc.at[k, n, 0:8, cc])
        if k == 0:
            for n in range(2, 5):
                state_load(c, n).wait()
        gossip(k, c).wait_recv()
        arrived(i, 5, re.at[k, :, cc])
        mine = raw(i, x, y)
        for h, rows in enumerate((low, high)):
            near = rx[k, 1 - h, 16:24, cc]
            mean = (mine[rows] + rc[k, h, 0:8, cc] + near + re[k, rows, cc]) * (1.0 / shards)
            track = 0.5 * (tw[k, 0, rows, cc] + twr[k, 0, rows, cc]) + mean - state[0, rows, cc]
            mix = 0.5 * (tw[k, 1, rows, cc] + twr[k, 1, rows, cc])
            if k + 1 < steps:
                one = BETA_ONE * state[1, rows, cc] + (1.0 - BETA_ONE) * track
                two = BETA_TWO * state[2, rows, cc] + (1.0 - BETA_TWO) * track * track
                tw[k + 1, 0, rows, cc] = track
                tw[k + 1, 1, rows, cc] = mix - LEARNING_RATE * one / (jnp.sqrt(two) + EPSILON)
                state[0, rows, cc] = mean
                state[1, rows, cc] = one
                state[2, rows, cc] = two
            else:
                last[0, rows, cc] = track
                last[1, rows, cc] = mix
        if k + 1 < steps:
            start_gossip(k + 1, c)
        if k + 2 == steps:
            result(c, 2).start()
            result(c, 3).start()
        if k + 1 == steps:
            result(c, 0).start()
            result(c, 1).start()

    def result(c, n):
        src = last.at[n, :, cols(c)] if n < 2 else state.at[n - 1, :, cols(c)]
        dst = (out_track, out_mix, out_one, out_two)[n].at[:, cols(c)]
        return pltpu.make_async_copy(src, dst, out_sem.at[c, n])

    every = range(len(chunks))
    grad_load(0).start()
    for c in every:
        state_load(c, 0).start()
        state_load(c, 1).start()
    for i in range(1, len(ITEMS)):
        grad_load(i).start()
    for c in every:
        for n in range(2, 5):
            state_load(c, n).start()

    phases = (None, phase_one, phase_two, phase_three, phase_four)
    fill(0)
    pl.semaphore_wait(barrier, len(feeders))
    for phase, i in PROGRAM:
        if phase == 0:
            state_load(i, 0).wait()
            state_load(i, 1).wait()
            start_gossip(0, i)
        elif phase == 5:
            relay(i)
        else:
            phases[phase](i)
            if phase == 1 and i + 1 < len(ITEMS):
                fill(i + 1)

    for c in every:
        for n in range(4):
            result(c, n).wait()
    for cp in sent:
        cp.wait_send()
    for k in range(steps):
        for c in every:
            gossip(k, c).wait_send()
            if hops[k] != shifts[k]:
                gossip(k, c, False).wait_send()


def finish(track, mix, first, second, params, change, one, two):
    one[...] = BETA_ONE * first[...] + (1.0 - BETA_ONE) * track[...]
    two[...] = BETA_TWO * second[...] + (1.0 - BETA_TWO) * track[...] * track[...]
    weights = mix[...] - LEARNING_RATE * one[...] / (jnp.sqrt(two[...]) + EPSILON)
    change[...] = (weights - params[...]) / LEARNING_RATE


def per_device(params, tracker, last_grad, first_moment, second_moment, local_grads):
    rows, width = params.shape[1:]
    steps = local_grads.shape[0]
    shards = lax.axis_size("fsdp")
    replicas = lax.axis_size("replica")
    chunks = [(sum(WIDTHS[:c]), w) for c, w in enumerate(WIDTHS)]
    assert sum(WIDTHS) == width and len(ITEMS) == steps * len(WIDTHS)
    count = len(ITEMS)
    f32 = jnp.float32
    any_spec = pl.BlockSpec(memory_space=pl.ANY)
    track, mix, one, two = pl.pallas_call(
        functools.partial(kernel, steps, replicas, shards, chunks),
        out_shape=(jax.ShapeDtypeStruct((rows, width), f32),) * 4,
        in_specs=[any_spec] * 6,
        out_specs=(any_spec,) * 4,
        scratch_shapes=[
            pltpu.VMEM((steps, shards, rows, width), jnp.bfloat16),
            pltpu.VMEM((3, rows, width), f32),
            pltpu.VMEM((steps, 2, rows, width), f32),
            pltpu.VMEM((steps, 2, rows, width), f32),
            pltpu.VMEM((2, rows, width), f32),
            pltpu.VMEM((steps, 16, width), f32),
            pltpu.VMEM((steps, 2, 32, width), f32),
            pltpu.VMEM((steps, 16, width), f32),
            pltpu.VMEM((steps, 16, width), f32),
            pltpu.VMEM((steps, 2, 32, width), f32),
            pltpu.VMEM((steps, 2, 8, width), f32),
            pltpu.VMEM((steps, 16, width), f32),
            pltpu.VMEM((steps, 2, 16, width), f32),
            pltpu.SemaphoreType.DMA((count,)),
            pltpu.SemaphoreType.DMA((len(chunks), 5)),
            pltpu.SemaphoreType.DMA((len(chunks), 4)),
            pltpu.SemaphoreType.DMA((count, 8)),
            pltpu.SemaphoreType.DMA((count, 8)),
            pltpu.SemaphoreType.DMA((steps, len(chunks))),
            pltpu.SemaphoreType.DMA((steps, len(chunks))),
            pltpu.VMEM((1, 2, rows, width), f32),
            pltpu.SemaphoreType.DMA((steps, len(chunks))),
            pltpu.SemaphoreType.DMA((steps, len(chunks))),
        ],
        compiler_params=pltpu.CompilerParams(
            collective_id=0, has_side_effects=True, vmem_limit_bytes=60 << 20
        ),
        name="gossip_window",
    )(
        params[0], tracker[0], last_grad[0], first_moment[0], second_moment[0],
        local_grads.reshape(steps, shards, rows, width),
    )
    tile = pl.BlockSpec((rows, width // FINISH_TILES), lambda c: (0, c))
    block = jax.ShapeDtypeStruct((rows, width), f32)
    change, one, two = pl.pallas_call(
        finish,
        grid=(FINISH_TILES,),
        out_shape=(block,) * 3,
        in_specs=[tile] * 5,
        out_specs=(tile,) * 3,
        name="finish",
    )(track, mix, one, two, params[0])
    return change[None], one[None], two[None]


def solution(mesh):
    in_specs = (P("replica", "fsdp", None),) * 5 + (P(None, "replica", "fsdp", None, None),)
    out_specs = (P("replica", "fsdp", None),) * 3
    return jax.shard_map(
        per_device, mesh=mesh, in_specs=in_specs, out_specs=out_specs, check_vma=False
    )
```

time: 235 us -> 95 us (0.40)
  waiting for transfers between devices: 191 us -> 0 us
  Pallas kernels: 0 us -> 94.3 us
  starting transfers between devices: 15.6 us -> 0 us
  other arithmetic: 14.8 us -> 0 us
  between operations: 13.8 us -> 0.64 us
    reduce_scatter x4 -> x0, waiting for transfers between devices: 167 us -> none  [per_device(): lax.psum_scatter(local_grads[iteration, 0, 0].astype(jnp.float32), 'fsdp'...]
    pallas_call x0 -> x2, Pallas kernels: none -> 94.3 us  [the longest x1 91.9 us: per_device(): pl.pallas_call(functools.partial(kernel, steps, replicas, shards, chunks)...]
    ppermute x8 -> x0, waiting for transfers between devices: 21.6 us -> none  [shifted(): return lax.ppermute(value, axis, pairs)]
    ppermute x8 -> x0, starting transfers between devices: 15.5 us -> none  [shifted(): return lax.ppermute(value, axis, pairs)]
    convert_element_type x1 -> x0, other arithmetic: 6.86 us -> none  [per_device(): local_grads[iteration, 0, 0].astype(jnp.float32)]
    sub x4 -> x0, other arithmetic: 4.02 us -> none  [the longest x3 2.98 us: per_device(): weights - LEARNING_RATE * moment_one / (jnp.sqrt(moment_two) + EPSILON)]
    broadcast_in_dim x3 -> x0, other arithmetic: 3.94 us -> none  [per_device(): return (change[None], moment_one[None], moment_two[None])]
  transfers between devices with their start and end apart: 12 -> 0, of which waited for: 7 -> 0; matrix products, arithmetic and copies ran while one was open for 3% -> 0% of each run, Pallas kernels for 0% -> 0%
where the time goes in v2:
time: 95 us; the launch traced here: 94.9 us
  Pallas kernels  94.3 us (99%)
    pallas_call x1, Pallas kernels, per_device(): pl.pallas_call(functools.partial(kernel, steps, replicas, shards, chunks)...  91.9 us
    pallas_call x1, Pallas kernels, per_device(): pl.pallas_call(finish, grid=(FINISH_TILES,), out_shape=(block,) * 3, in_s...  2.33 us

profile of v2, /device:TPU:16, one launch (start us, length us, event | category | flops | bytes accessed | tf_op | source)
XLA Modules:
  0.0 94.9 jit_solution(17035567805561328430)
XLA Ops:
  0.6 91.9 %gossip_window.1 = (f32[16,5120]{1,0:T(8,128)}, f32[16,5120]{1,0:T(8,128)}, f32[16,5120]{1,0:T(8,128)}, f32[16,5120]{1,0:T(8,128)}) custom-call(f32[16,5120]{1,0:T(8,128)} %bitcast.10, f32[16,5120]{1,0:T(8,128)} %bitcast.12, f32[16,5120]{1,0:T(8,128)} %bitcast.13, f32[16,5120]{1,0:T(8,128)} %bitcast.14, f32[16,5120]{1,0:T(8,128)} %bitcast.15, ...), custom_call_target="tpu_custom_call" | custom-call | tf_op jit(solution)/shard_map/gossip_window/pallas_call | solution.py:284
  92.6 2.3 %finish.1 = (f32[16,5120]{1,0:T(8,128)}, f32[16,5120]{1,0:T(8,128)}, f32[16,5120]{1,0:T(8,128)}) custom-call(f32[16,5120]{1,0:T(8,128)} %get-tuple-element.10.track, f32[16,5120]{1,0:T(8,128)} %get-tuple-element.11.mix, f32[16,5120]{1,0:T(8,128)} %get-tuple-element.12.first, f32[16,5120]{1,0:T(8,128)} %get-tuple-element.13.second, f32[16,5120]{1,0:T(8,128)} %bitcast.11), custom_call_target="tpu_custom_call" | custom-call | tf_op jit(solution)/shard_map/finish/pallas_call | solution.py:324

commit v3 on v2

--- a/solution.py
+++ b/solution.py
@@ -17,19 +17,19 @@
 NX = 4
 WIDTHS = [1152, 1152, 1024, 1024, 768]
 ITEMS = [
-    (0, 4), (0, 2), (1, 4), (2, 4), (1, 2), (2, 2), (0, 1), (0, 0), (1, 1), (0, 3), (2, 1), (1, 0), (1, 3),
-    (2, 3), (2, 0), (3, 2), (3, 0), (3, 1), (3, 4), (3, 3),
+    (0, 4), (1, 4), (0, 3), (1, 3), (2, 4), (0, 0), (2, 3), (0, 1), (1, 0), (0, 2), (2, 0), (1, 1), (1, 2),
+    (2, 1), (2, 2), (3, 0), (3, 4), (3, 1), (3, 3), (3, 2),
 ]
-X_FIRST = [4, 5, 11]
+X_FIRST = [5, 8, 4]
 PROGRAM = [
-    (0, 2), (1, 0), (1, 1), (1, 2), (1, 3), (0, 4), (0, 1), (2, 0), (0, 3), (2, 1), (1, 4), (3, 0), (2, 2),
-    (3, 1), (2, 4), (1, 5), (1, 6), (4, 0), (3, 2), (4, 1), (2, 5), (3, 4), (2, 3), (0, 0), (2, 6), (1, 7),
-    (4, 2), (3, 5), (3, 3), (3, 6), (4, 4), (1, 8), (1, 9), (4, 3), (2, 7), (4, 6), (1, 10), (4, 5), (2, 8),
-    (3, 7), (5, 4), (2, 9), (1, 11), (4, 7), (3, 8), (2, 10), (3, 9), (2, 11), (1, 12), (5, 2), (4, 8), (3,
-    10), (1, 13), (3, 11), (1, 14), (4, 9), (2, 12), (4, 10), (1, 15), (4, 11), (2, 14), (3, 12), (2, 13), (1,
-    16), (5, 1), (3, 14), (1, 17), (3, 13), (4, 12), (1, 18), (2, 15), (4, 14), (1, 19), (4, 13), (2, 18), (2,
-    16), (2, 17), (5, 0), (3, 15), (2, 19), (3, 16), (5, 3), (3, 17), (3, 18), (4, 15), (3, 19), (4, 16), (4,
-    17), (4, 18), (4, 19),
+    (1, 0), (1, 1), (1, 2), (0, 4), (0, 3), (2, 0), (1, 3), (2, 2), (2, 1), (3, 0), (1, 4), (0, 2), (3, 2),
+    (1, 5), (2, 3), (4, 0), (4, 2), (2, 4), (3, 1), (2, 5), (1, 6), (0, 0), (3, 3), (1, 7), (4, 1), (3, 4),
+    (3, 5), (0, 1), (2, 6), (1, 8), (4, 3), (4, 4), (3, 6), (2, 7), (1, 9), (2, 8), (4, 5), (4, 6), (3, 7),
+    (5, 4), (1, 10), (3, 8), (2, 9), (1, 11), (4, 7), (2, 10), (1, 12), (4, 8), (3, 9), (2, 11), (3, 10), (5,
+    3), (1, 13), (4, 9), (3, 11), (1, 14), (4, 10), (2, 12), (1, 15), (4, 11), (2, 13), (3, 12), (1, 16), (5,
+    0), (2, 14), (3, 13), (1, 17), (4, 12), (3, 14), (1, 18), (4, 13), (1, 19), (2, 15), (2, 16), (4, 14), (2,
+    18), (2, 17), (5, 1), (2, 19), (3, 15), (3, 16), (5, 2), (3, 18), (3, 17), (3, 19), (4, 15), (4, 16), (4,
+    18), (4, 17), (4, 19),
 ]
 FINISH_TILES = 2
 

time: 95 us -> 93.9 us (0.988)
  Pallas kernels: 94.3 us -> 93.1 us
    pallas_call x1, Pallas kernels: 91.9 us -> 90.8 us  [per_device(): pl.pallas_call(functools.partial(kernel, steps, replicas, shards, chunks)...]
where the time goes in v3:
time: 93.9 us; the launch traced here: 93.8 us
  Pallas kernels  93.1 us (99%)
    pallas_call x1, Pallas kernels, per_device(): pl.pallas_call(functools.partial(kernel, steps, replicas, shards, chunks)...  90.8 us
    pallas_call x1, Pallas kernels, per_device(): pl.pallas_call(finish, grid=(FINISH_TILES,), out_shape=(block,) * 3, in_s...  2.33 us

profile of v3, /device:TPU:16, one launch (start us, length us, event | category | flops | bytes accessed | tf_op | source)
XLA Modules:
  0.0 93.8 jit_solution(2843601419687921469)
XLA Ops:
  0.6 90.8 %gossip_window.1 = (f32[16,5120]{1,0:T(8,128)}, f32[16,5120]{1,0:T(8,128)}, f32[16,5120]{1,0:T(8,128)}, f32[16,5120]{1,0:T(8,128)}) custom-call(f32[16,5120]{1,0:T(8,128)} %bitcast.10, f32[16,5120]{1,0:T(8,128)} %bitcast.12, f32[16,5120]{1,0:T(8,128)} %bitcast.13, f32[16,5120]{1,0:T(8,128)} %bitcast.14, f32[16,5120]{1,0:T(8,128)} %bitcast.15, ...), custom_call_target="tpu_custom_call" | custom-call | tf_op jit(solution)/shard_map/gossip_window/pallas_call | solution.py:284
  91.4 2.3 %finish.1 = (f32[16,5120]{1,0:T(8,128)}, f32[16,5120]{1,0:T(8,128)}, f32[16,5120]{1,0:T(8,128)}) custom-call(f32[16,5120]{1,0:T(8,128)} %get-tuple-element.10.track, f32[16,5120]{1,0:T(8,128)} %get-tuple-element.11.mix, f32[16,5120]{1,0:T(8,128)} %get-tuple-element.12.first, f32[16,5120]{1,0:T(8,128)} %get-tuple-element.13.second, f32[16,5120]{1,0:T(8,128)} %bitcast.11), custom_call_target="tpu_custom_call" | custom-call | tf_op jit(solution)/shard_map/finish/pallas_call | solution.py:324

commit v4 on v2

--- a/solution.py
+++ b/solution.py
@@ -17,18 +17,18 @@
 NX = 4
 WIDTHS = [1152, 1152, 1024, 1024, 768]
 ITEMS = [
-    (0, 4), (0, 2), (1, 4), (2, 4), (1, 2), (2, 2), (0, 1), (0, 0), (1, 1), (0, 3), (2, 1), (1, 0), (1, 3),
-    (2, 3), (2, 0), (3, 2), (3, 0), (3, 1), (3, 4), (3, 3),
+    (0, 1), (0, 3), (1, 1), (1, 3), (2, 1), (0, 2), (2, 3), (0, 0), (1, 2), (0, 4), (1, 0), (2, 2), (1, 4),
+    (2, 0), (2, 4), (3, 2), (3, 1), (3, 0), (3, 3), (3, 4),
 ]
-X_FIRST = [4, 5, 11]
+X_FIRST = [5, 3, 11, 6]
 PROGRAM = [
-    (0, 2), (1, 0), (1, 1), (1, 2), (1, 3), (0, 4), (0, 1), (2, 0), (0, 3), (2, 1), (1, 4), (3, 0), (2, 2),
-    (3, 1), (2, 4), (1, 5), (1, 6), (4, 0), (3, 2), (4, 1), (2, 5), (3, 4), (2, 3), (0, 0), (2, 6), (1, 7),
-    (4, 2), (3, 5), (3, 3), (3, 6), (4, 4), (1, 8), (1, 9), (4, 3), (2, 7), (4, 6), (1, 10), (4, 5), (2, 8),
-    (3, 7), (5, 4), (2, 9), (1, 11), (4, 7), (3, 8), (2, 10), (3, 9), (2, 11), (1, 12), (5, 2), (4, 8), (3,
-    10), (1, 13), (3, 11), (1, 14), (4, 9), (2, 12), (4, 10), (1, 15), (4, 11), (2, 14), (3, 12), (2, 13), (1,
-    16), (5, 1), (3, 14), (1, 17), (3, 13), (4, 12), (1, 18), (2, 15), (4, 14), (1, 19), (4, 13), (2, 18), (2,
-    16), (2, 17), (5, 0), (3, 15), (2, 19), (3, 16), (5, 3), (3, 17), (3, 18), (4, 15), (3, 19), (4, 16), (4,
+    (1, 0), (0, 0), (1, 1), (1, 2), (2, 0), (1, 3), (0, 1), (0, 3), (2, 1), (3, 0), (1, 4), (2, 2), (3, 1),
+    (4, 0), (0, 4), (1, 5), (2, 3), (3, 2), (4, 1), (2, 4), (1, 6), (2, 5), (3, 3), (0, 2), (4, 2), (3, 4),
+    (2, 6), (1, 7), (1, 8), (4, 3), (3, 5), (4, 4), (1, 9), (3, 6), (2, 7), (1, 10), (4, 5), (2, 8), (4, 6),
+    (3, 7), (2, 9), (1, 11), (5, 1), (3, 8), (2, 10), (4, 7), (1, 12), (2, 11), (5, 3), (3, 9), (3, 10), (1,
+    13), (1, 14), (4, 8), (3, 11), (4, 9), (2, 12), (4, 10), (2, 13), (1, 15), (3, 12), (4, 11), (2, 14), (3,
+    13), (1, 16), (4, 12), (1, 17), (3, 14), (2, 15), (4, 13), (1, 18), (5, 2), (1, 19), (4, 14), (2, 16), (2,
+    17), (5, 0), (2, 18), (2, 19), (3, 15), (3, 16), (3, 17), (5, 4), (3, 18), (3, 19), (4, 15), (4, 16), (4,
     17), (4, 18), (4, 19),
 ]
 FINISH_TILES = 2

time: 95 us -> 93.5 us (0.984)
  Pallas kernels: 94.3 us -> 92.6 us
    pallas_call x1, Pallas kernels: 91.9 us -> 90.3 us  [per_device(): pl.pallas_call(functools.partial(kernel, steps, replicas, shards, chunks)...]
where the time goes in v4:
time: 93.5 us; the launch traced here: 93.3 us
  Pallas kernels  92.6 us (99%)
    pallas_call x1, Pallas kernels, per_device(): pl.pallas_call(functools.partial(kernel, steps, replicas, shards, chunks)...  90.3 us
    pallas_call x1, Pallas kernels, per_device(): pl.pallas_call(finish, grid=(FINISH_TILES,), out_shape=(block,) * 3, in_s...  2.33 us

profile of v4, /device:TPU:16, one launch (start us, length us, event | category | flops | bytes accessed | tf_op | source)
XLA Modules:
  0.0 93.3 jit_solution(6725424155115332348)
XLA Ops:
  0.6 90.3 %gossip_window.1 = (f32[16,5120]{1,0:T(8,128)}, f32[16,5120]{1,0:T(8,128)}, f32[16,5120]{1,0:T(8,128)}, f32[16,5120]{1,0:T(8,128)}) custom-call(f32[16,5120]{1,0:T(8,128)} %bitcast.10, f32[16,5120]{1,0:T(8,128)} %bitcast.12, f32[16,5120]{1,0:T(8,128)} %bitcast.13, f32[16,5120]{1,0:T(8,128)} %bitcast.14, f32[16,5120]{1,0:T(8,128)} %bitcast.15, ...), custom_call_target="tpu_custom_call" | custom-call | tf_op jit(solution)/shard_map/gossip_window/pallas_call | solution.py:284
  90.9 2.3 %finish.1 = (f32[16,5120]{1,0:T(8,128)}, f32[16,5120]{1,0:T(8,128)}, f32[16,5120]{1,0:T(8,128)}) custom-call(f32[16,5120]{1,0:T(8,128)} %get-tuple-element.10.track, f32[16,5120]{1,0:T(8,128)} %get-tuple-element.11.mix, f32[16,5120]{1,0:T(8,128)} %get-tuple-element.12.first, f32[16,5120]{1,0:T(8,128)} %get-tuple-element.13.second, f32[16,5120]{1,0:T(8,128)} %bitcast.11), custom_call_target="tpu_custom_call" | custom-call | tf_op jit(solution)/shard_map/finish/pallas_call | solution.py:324
